TPU v7x, 32 devices: a whole 2x2x4 slice. The times are simulated.
32 devices in a mesh: groups: 2 (over y), wide: 4 (over z), tail: 2 (over x), sub: 2 (over core).
Axes of the slice: x: 2, y: 2, z: 4, core: 2. Of those that a mesh axis runs over, the one named last changes fastest.
Arguments:
- head_embed: float32 [512, 512], P(('groups', 'wide')), parts along dimension 0, may hold values from -2.1 to 2.1
- tail_embed: float32 [512, 512], P(('groups', 'tail'), 'sub'), parts along dimension 0, may hold values from -2.1 to 2.1
- core_mats: float32 [8, 512, 512], P(('groups', 'wide'), None, 'sub'), parts along dimension 0, may hold values from -0.25 to 0.25
- labels: int32 [512, 8, 256], P(('groups', 'wide'), None, 'tail'), parts along dimension 0, may hold values 0 or 1
- core_lists: int32 [4, 8], P(('groups', 'tail')), parts along dimension 0, may hold values from 0 to 3, as said below
Outputs:
- grad_head: float32 [512, 512], P(('groups', 'wide', 'tail', 'sub')), parts along dimension 0
- grad_tail: float32 [4, 128, 512], P(('groups', 'tail'), 'wide', 'sub'), parts along dimension 0
- grad_cores: float32 [8, 512, 512], P(('groups', 'tail'), 'wide', 'sub'), parts along dimension 0
There are 2 independent parts, one for each index of `groups`. A program takes and returns all parts, laid end to end along the dimension named above; each array names one. Nothing has to cross between parts.
Inputs may be any that keep to these rules, and one draw needn't show every extreme that they name: `core_lists`: every one of the 4 core ids stands somewhere in the lists; ids may repeat.
All inputs are finite; a program needn't handle non-finite values. No bound on the sum of `labels` on one device may be relied on, other than what follows from the above.
Results may differ from a plain program's by a relative error of at most 0.0001.
Values sent between devices are 32-bit elements; how exact they have to be, the bound alone decides.
A program may use at most 64 MiB of HBM per device.

v0:
```python
import math

import jax
import jax.numpy as jnp
from jax import lax
from jax.sharding import PartitionSpec as P


def broadcast(value, axis, source):
    kept = jnp.where(lax.axis_index(axis) == source, value, 0).astype(value.dtype)
    return lax.psum(kept, axis)


def body(head_embed, tail_embed, core_mats, labels, core_lists):
    highest = lax.Precision.HIGHEST
    slot_count = core_lists.shape[1]
    half_width = tail_embed.shape[1]
    listed = core_lists[0]
    wide_count = lax.axis_size("wide")
    tail_acc = jnp.zeros((tail_embed.shape[0], half_width), jnp.float32)
    head_acc = jnp.zeros(head_embed.shape, jnp.float32)
    core_terms = []
    for slot_index in range(slot_count):
        relation = listed[slot_index]
        owned_count = core_mats.shape[0]
        local_core = lax.dynamic_index_in_dim(core_mats, relation % owned_count, 0, keepdims=False)
        matrix = broadcast(local_core, "wide", relation // owned_count)
        projected = jnp.dot(
            head_embed, matrix, precision=highest, preferred_element_type=jnp.float32
        )
        partial_score = lax.dot_general(
            projected, tail_embed, (((1,), (1,)), ((), ())), precision=highest
        )
        score_tile = lax.psum(partial_score, "sub")
        residual = jax.nn.sigmoid(score_tile) - labels[:, slot_index, :].astype(jnp.float32)
        tail_acc = tail_acc + lax.dot_general(
            residual, projected, (((0,), (0,)), ((), ())), precision=highest
        )
        weighted = jnp.dot(
            residual, tail_embed, precision=highest, preferred_element_type=jnp.float32
        )
        head_acc = head_acc + lax.dot_general(
            weighted, matrix, (((1,), (1,)), ((), ())), precision=highest
        )
        core_term = lax.dot_general(
            head_embed, weighted, (((0,), (0,)), ((), ())), precision=highest
        )
        core_terms.append(core_term)
    core_rows, tail_stack = (
        lax.psum_scatter(jnp.stack(core_terms), "wide", scatter_dimension=1, tiled=True),
        lax.psum_scatter(tail_acc[None], "wide", scatter_dimension=1, tiled=True),
    )
    tail_part = tail_stack[0]
    relation_count = core_mats.shape[0] * wide_count
    selector = (jnp.arange(relation_count, dtype=jnp.int32)[:, None] == listed[None, :]).astype(
        jnp.float32
    )
    combined = jnp.einsum("rj,jab->rab", selector, core_rows, precision=highest)
    heads_total = head_embed.shape[0] * wide_count
    tails_total = tail_embed.shape[0] * lax.axis_size("tail")
    core_grad = lax.psum_scatter(combined, "tail", scatter_dimension=0, tiled=True) * (
        1.0 / math.sqrt(heads_total * tail_embed.shape[0])
    )
    head_grad = lax.psum_scatter(head_acc, ("tail", "sub"), scatter_dimension=0, tiled=True) * (
        1.0 / math.sqrt(slot_count * tails_total)
    )
    tail_grad = (tail_part * (1.0 / math.sqrt(slot_count * heads_total)))[None]
    return (head_grad, tail_grad, core_grad)


def solution(mesh):
    in_specs = (
        P(("groups", "wide"), None),
        P(("groups", "tail"), "sub"),
        P(("groups", "wide"), None, "sub"),
        P(("groups", "wide"), None, "tail"),
        P(("groups", "tail"), None),
    )
    out_specs = (
        P(("groups", "wide", "tail", "sub"), None),
        P(("groups", "tail"), "wide", "sub"),
        P(("groups", "tail"), "wide", "sub"),
    )
    return jax.shard_map(body, mesh=mesh, in_specs=in_specs, out_specs=out_specs, check_vma=False)
```

profile of v0, /device:TPU:0, one launch (start us, length us, event | category | flops | bytes accessed | tf_op | source)
XLA Modules:
  0.0 376.8 jit_solution(4680497996379933882)
XLA Ops:
  7.2 1.6 fusion.23
  13.9 3.2 select_bitcast_fusion
  17.2 160.3 %all-reduce.5.cloned.1.call-done = (f32[512,256]{1,0:T(8,128)}, f32[512,256]{1,0:T(8,128)}, f32[512,256]{1,0:T(8,128)}, f32[512,256]{1,0:T(8,128)}, f32[512,256]...) async-done(((f32[512,256]{1,0:T(8,128)}, f32[512,256]{1,0:T(8,128)}, f32[512,256]{1,0:T(8,128)}, f32[512,256]{1,0:T(8,128)}, ...) | async-done | bytes 4194320 | tf_op jit(solution)/shard_map/psum | solution.py:11
  177.5 1.6 fusion.24
  179.1 1.5 fusion.27
  180.6 0.9 fusion.25
  182.4 1.5 fusion.29
  183.9 0.9 fusion.30
  184.8 1.5 fusion.31
  187.1 1.5 fusion.33
  193.7 17.4 %all-reduce.7.cloned.1.call-done = (f32[64,128]{1,0:T(8,128)}, f32[64,128]{1,0:T(8,128)}, f32[64,128]{1,0:T(8,128)}, f32[64,128]{1,0:T(8,128)}, f32[64,128]{1,0:...) async-done(((f32[64,128]{1,0:T(8,128)}, f32[64,128]{1,0:T(8,128)}, f32[64,128]{1,0:T(8,128)}, f32[64,128]{1,0:T(8,128)}, f32[64,128]{1,0:T(8,128)}, ...) | async-done | bytes 262160 | tf_op jit(solution)/shard_map/psum | solution.py:34
  211.1 1.0 fusion.14
  212.1 1.4 fusion.7
  213.6 1.0 fusion.21
  214.6 1.0 fusion.20
  215.6 1.0 fusion.19
  216.6 1.0 fusion.18
  217.6 1.0 fusion.17
  218.6 1.0 fusion.16
  219.6 1.0 fusion.15
  220.6 1.5 fusion.6
  222.1 1.4 fusion.5
  223.5 1.4 fusion.4
  225.0 1.4 fusion.3
  226.4 1.4 fusion.2
  227.9 1.4 fusion.1
  229.3 1.4 fusion
  231.1 1.3 fusion.13
  232.4 1.2 convolution_add_fusion.13
  233.6 1.2 convolution_add_fusion.12
  234.8 1.2 convolution_add_fusion.11
  236.0 1.1 convolution_add_fusion.10
  237.1 1.8 convolution_add_fusion.9
  238.9 1.7 fusion.26
  240.6 1.7 convolution_add_fusion.6
  242.3 1.5 convolution_add_fusion.5
  246.3 1.3 convolution_add_fusion
  247.6 1.1 convolution_add_fusion.8
  248.7 1.8 fusion.8
  250.6 58.4 %reduce-scatter.9.cloned.1.call-done = f32[8,128,256]{1,2,0:T(8,128)} async-done(((f32[8,512,256]{1,2,0:T(8,128)}), f32[8,128,256]{1,2,0:T(8,128)}) %reduce-scatter.9.cloned.1.call-update) | async-done | bytes 1048592 | tf_op jit(solution)/shard_map/reduce_scatter | solution.py:50
  308.9 1.7 copy.26
  311.2 0.9 copy.27
  312.2 19.8 %reduce-scatter.5.cloned.1.call-done = f32[16,512]{1,0:T(8,128)} async-done(((f32[64,512]{1,0:T(8,128)}), f32[16,512]{1,0:T(8,128)}) %reduce-scatter.5.cloned.1.call-update) | async-done | bytes 32784 | tf_op jit(solution)/shard_map/reduce_scatter | solution.py:64
  332.0 1.4 broadcast_multiply_fusion.2
  333.4 19.9 %reduce-scatter.7.cloned.1.call-done = f32[1,32,256]{2,1,0:T(8,128)} async-done(((f32[1,128,256]{2,1,0:T(8,128)}), f32[1,32,256]{2,1,0:T(8,128)}) %reduce-scatter.7.cloned.1.call-update) | async-done | bytes 32784 | tf_op jit(solution)/shard_map/reduce_scatter | solution.py:51
  353.3 1.4 broadcast_multiply_fusion.1
  354.7 13.6 %reduce-scatter.11.cloned.1.call-done = f32[2,128,256]{2,1,0:T(8,128)} async-done(((f32[4,128,256]{2,1,0:T(8,128)}), f32[2,128,256]{2,1,0:T(8,128)}) %reduce-scatter.11.cloned.1.call-update) | async-done | bytes 262160 | tf_op jit(solution)/shard_map/reduce_scatter | solution.py:61
  368.3 1.7 broadcast_multiply_fusion
  (107 shorter events, 10.4 us)
Async XLA Ops:
  7.2 170.4 %copy-start = (f32[64,512]{1,0:T(8,128)S(1)}, f32[64,512]{1,0:T(8,128)}, u32[]{:S(2)}) copy-start(f32[64,512]{1,0:T(8,128)} %param.5) | copy-start | bytes 393220
  7.2 170.3 %all-reduce.5.cloned.1.call-start = ((), (), s32[]{:S(2)}) async-start(), calls=%async_computation.8 | async-start | bytes 8388608 | tf_op jit(solution)/shard_map/psum | solution.py:11
  13.9 166.7 %copy-start.1 = (f32[128,256]{1,0:T(8,128)S(1)}, f32[128,256]{1,0:T(8,128)}, u32[]{:S(2)}) copy-start(f32[128,256]{1,0:T(8,128)} %param.6) | copy-start | bytes 393220
  17.1 176.3 %copy-start.38 = (s32[64,8,128]{2,1,0:T(8,128)S(1)}, s32[64,8,128]{2,1,0:T(8,128)}, u32[]{:S(2)}) copy-start(s32[64,8,128]{2,1,0:T(8,128)} %param.8) | copy-start | bytes 786436
  17.1 194.0 %all-reduce.7.cloned.1.call-start = ((), (), s32[]{:S(2)}) async-start(), calls=%async_computation.9 | async-start | bytes 524288 | tf_op jit(solution)/shard_map/psum | solution.py:34
  177.5 12.0 %copy-start.4 = (f32[512,256]{1,0:T(8,128)S(1)}, f32[512,256]{1,0:T(8,128)}, u32[]{:S(2)}) copy-start(f32[512,256]{1,0:T(8,128)} %get-tuple-element.11) | copy-start | bytes 1572868
  177.5 13.3 %copy-start.3 = (f32[512,256]{1,0:T(8,128)S(1)}, f32[512,256]{1,0:T(8,128)}, u32[]{:S(2)}) copy-start(f32[512,256]{1,0:T(8,128)} %get-tuple-element.12) | copy-start | bytes 1572868
  177.5 14.6 %copy-start.2 = (f32[512,256]{1,0:T(8,128)S(1)}, f32[512,256]{1,0:T(8,128)}, u32[]{:S(2)}) copy-start(f32[512,256]{1,0:T(8,128)} %get-tuple-element.13) | copy-start | bytes 1572868
  179.1 13.0 %copy-start.15 = (f32[256,64]{0,1:T(8,128)}, f32[256,64]{0,1:T(8,128)S(1)}, u32[]{:S(2)}) copy-start(f32[256,64]{0,1:T(8,128)S(1)} %fusion.24) | copy-start | bytes 196612
  180.6 1.8 copy-start.14
  183.9 0.9 copy-start.13
  186.2 0.9 copy-start.12
  188.6 0.9 copy-start.10
  189.9 2.2 copy-start.8
  193.4 115.5 %reduce-scatter.9.cloned.1.call-start = ((), (), s32[]{:S(2)}) async-start(), calls=%async_computation.6 | async-start | bytes 5242880 | tf_op jit(solution)/shard_map/reduce_scatter | solution.py:50
  193.7 34.2 %copy-start.30 = (s32[64,1,128]{2,1,0:T(1,128)}, s32[64,1,128]{2,1,0:T(1,128)S(1)}, u32[]{:S(2)}) copy-start(s32[64,1,128]{2,1,0:T(1,128)S(1)} %get-tuple-element.30) | copy-start | bytes 98308
  193.7 34.2 %copy-start.31 = (s32[64,1,128]{2,1,0:T(1,128)}, s32[64,1,128]{2,1,0:T(1,128)S(1)}, u32[]{:S(2)}) copy-start(s32[64,1,128]{2,1,0:T(1,128)S(1)} %get-tuple-element.31) | copy-start | bytes 98308
  193.7 34.1 %copy-start.32 = (s32[64,1,128]{2,1,0:T(1,128)}, s32[64,1,128]{2,1,0:T(1,128)S(1)}, u32[]{:S(2)}) copy-start(s32[64,1,128]{2,1,0:T(1,128)S(1)} %get-tuple-element.32) | copy-start | bytes 98308
  193.7 34.1 %copy-start.33 = (s32[64,1,128]{2,1,0:T(1,128)}, s32[64,1,128]{2,1,0:T(1,128)S(1)}, u32[]{:S(2)}) copy-start(s32[64,1,128]{2,1,0:T(1,128)S(1)} %get-tuple-element.33) | copy-start | bytes 98308
  193.7 34.1 %copy-start.34 = (s32[64,1,128]{2,1,0:T(1,128)}, s32[64,1,128]{2,1,0:T(1,128)S(1)}, u32[]{:S(2)}) copy-start(s32[64,1,128]{2,1,0:T(1,128)S(1)} %get-tuple-element.34) | copy-start | bytes 98308
  193.7 34.1 %copy-start.35 = (s32[64,1,128]{2,1,0:T(1,128)}, s32[64,1,128]{2,1,0:T(1,128)S(1)}, u32[]{:S(2)}) copy-start(s32[64,1,128]{2,1,0:T(1,128)S(1)} %get-tuple-element.35) | copy-start | bytes 98308
  193.7 34.1 %copy-start.36 = (s32[64,1,128]{2,1,0:T(1,128)}, s32[64,1,128]{2,1,0:T(1,128)S(1)}, u32[]{:S(2)}) copy-start(s32[64,1,128]{2,1,0:T(1,128)S(1)} %get-tuple-element.36) | copy-start | bytes 98308
  193.7 34.1 %copy-start.37 = (s32[64,1,128]{2,1,0:T(1,128)}, s32[64,1,128]{2,1,0:T(1,128)S(1)}, u32[]{:S(2)}) copy-start(s32[64,1,128]{2,1,0:T(1,128)S(1)} %get-tuple-element.37) | copy-start | bytes 98308
  212.1 1.4 copy-start.26
  214.5 14.8 %copy-start.16 = (f32[64,256]{1,0:T(8,128)}, f32[64,256]{1,0:T(8,128)S(1)}, u32[]{:S(2)}) copy-start(f32[64,256]{1,0:T(8,128)S(1)} %fusion.21) | copy-start | bytes 196612
  215.6 12.3 %copy-start.18 = (f32[64,256]{1,0:T(8,128)}, f32[64,256]{1,0:T(8,128)S(1)}, u32[]{:S(2)}) copy-start(f32[64,256]{1,0:T(8,128)S(1)} %fusion.20) | copy-start | bytes 196612
  216.6 12.7 %copy-start.20 = (f32[64,256]{1,0:T(8,128)}, f32[64,256]{1,0:T(8,128)S(1)}, u32[]{:S(2)}) copy-start(f32[64,256]{1,0:T(8,128)S(1)} %fusion.19) | copy-start | bytes 196612
  217.6 11.7 %copy-start.22 = (f32[64,256]{1,0:T(8,128)}, f32[64,256]{1,0:T(8,128)S(1)}, u32[]{:S(2)}) copy-start(f32[64,256]{1,0:T(8,128)S(1)} %fusion.18) | copy-start | bytes 196612
  218.6 10.7 %copy-start.24 = (f32[64,256]{1,0:T(8,128)}, f32[64,256]{1,0:T(8,128)S(1)}, u32[]{:S(2)}) copy-start(f32[64,256]{1,0:T(8,128)S(1)} %fusion.17) | copy-start | bytes 196612
  219.6 9.7 %copy-start.27 = (f32[64,256]{1,0:T(8,128)}, f32[64,256]{1,0:T(8,128)S(1)}, u32[]{:S(2)}) copy-start(f32[64,256]{1,0:T(8,128)S(1)} %fusion.16) | copy-start | bytes 196612
  220.6 8.7 %copy-start.28 = (f32[64,256]{1,0:T(8,128)}, f32[64,256]{1,0:T(8,128)S(1)}, u32[]{:S(2)}) copy-start(f32[64,256]{1,0:T(8,128)S(1)} %fusion.15) | copy-start | bytes 196612
  225.0 11.0 %copy-start.11 = (f32[256,64]{0,1:T(8,128)S(1)}, f32[256,64]{0,1:T(8,128)}, u32[]{:S(2)}) copy-start(f32[256,64]{0,1:T(8,128)} %copy-done.10) | copy-start | bytes 196612
  226.4 10.7 %copy-start.9 = (f32[256,64]{0,1:T(8,128)S(1)}, f32[256,64]{0,1:T(8,128)}, u32[]{:S(2)}) copy-start(f32[256,64]{0,1:T(8,128)} %copy-done.8) | copy-start | bytes 196612
  229.3 13.0 %copy-start.7 = (f32[512,256]{1,0:T(8,128)S(1)}, f32[512,256]{1,0:T(8,128)}, u32[]{:S(2)}) copy-start(f32[512,256]{1,0:T(8,128)} %get-tuple-element.8) | copy-start | bytes 1572868
  230.8 13.0 %copy-start.6 = (f32[512,256]{1,0:T(8,128)S(1)}, f32[512,256]{1,0:T(8,128)}, u32[]{:S(2)}) copy-start(f32[512,256]{1,0:T(8,128)} %get-tuple-element.9) | copy-start | bytes 1572868
  230.8 13.6 %copy-start.5 = (f32[512,256]{1,0:T(8,128)S(1)}, f32[512,256]{1,0:T(8,128)}, u32[]{:S(2)}) copy-start(f32[512,256]{1,0:T(8,128)} %get-tuple-element.10) | copy-start | bytes 1572868
  230.8 101.2 %reduce-scatter.5.cloned.1.call-start = ((), (), s32[]{:S(2)}) async-start(), calls=%async_computation.4 | async-start | bytes 163840 | tf_op jit(solution)/shard_map/reduce_scatter | solution.py:64
  231.0 12.8 %copy-start.25 = (f32[64,256]{1,0:T(8,128)S(1)}, f32[64,256]{1,0:T(8,128)}, u32[]{:S(2)}) copy-start(f32[64,256]{1,0:T(8,128)} %copy-done.24) | copy-start | bytes 196612
  231.0 13.4 %copy-start.23 = (f32[64,256]{1,0:T(8,128)S(1)}, f32[64,256]{1,0:T(8,128)}, u32[]{:S(2)}) copy-start(f32[64,256]{1,0:T(8,128)} %copy-done.22) | copy-start | bytes 196612
  231.0 14.0 %copy-start.21 = (f32[64,256]{1,0:T(8,128)S(1)}, f32[64,256]{1,0:T(8,128)}, u32[]{:S(2)}) copy-start(f32[64,256]{1,0:T(8,128)} %copy-done.20) | copy-start | bytes 196612
  231.1 14.6 %copy-start.19 = (f32[64,256]{1,0:T(8,128)S(1)}, f32[64,256]{1,0:T(8,128)}, u32[]{:S(2)}) copy-start(f32[64,256]{1,0:T(8,128)} %copy-done.18) | copy-start | bytes 196612
  231.1 15.2 %copy-start.17 = (f32[64,256]{1,0:T(8,128)S(1)}, f32[64,256]{1,0:T(8,128)}, u32[]{:S(2)}) copy-start(f32[64,256]{1,0:T(8,128)} %copy-done.16) | copy-start | bytes 196612
  238.9 8.7 %copy-start.29 = (f32[128,256]{1,0:T(8,128)S(1)}, f32[128,256]{1,0:T(8,128)}, u32[]{:S(2)}) copy-start(f32[128,256]{1,0:T(8,128)} %convolution_add_fusion.9) | copy-start | bytes 393220
  242.3 68.3 %copy-start.39 = (s32[1,8]{1,0:T(1,128)S(1)}, s32[1,8]{1,0:T(1,128)}, u32[]{:S(2)}) copy-start(s32[1,8]{1,0:T(1,128)} %param.9) | copy-start | bytes 100
  247.6 105.7 %reduce-scatter.7.cloned.1.call-start = ((), (), s32[]{:S(2)}) async-start(), calls=%async_computation.5 | async-start | bytes 163840 | tf_op jit(solution)/shard_map/reduce_scatter | solution.py:51
  250.5 117.8 %reduce-scatter.11.cloned.1.call-start = ((), (), s32[]{:S(2)}) async-start(), calls=%async_computation.7 | async-start | bytes 786432 | tf_op jit(solution)/shard_map/reduce_scatter | solution.py:61
Sparse Core Ops, SparseCore 0:
  17.2 160.2 all-reduce.4
  193.5 17.5 all-reduce.6
  230.9 77.9 reduce-scatter.8
  311.9 20.0 reduce-scatter.4
  334.1 19.1 reduce-scatter.6
  355.5 12.7 reduce-scatter.10
where the time goes:
time: 379 us; the launch traced here: 377 us
  waiting for transfers between devices  290 us (77%)
  matrix products  54.9 us (14%)
  between operations  19.7 us (5%)
  other arithmetic  7.64 us (2%)
  local copies, waits for them, and re-layouts  4.56 us (1%)
    psum x1, waiting for transfers between devices, broadcast(): return lax.psum(kept, axis)  160 us
    reduce_scatter x1, waiting for transfers between devices, body(): lax.psum_scatter(jnp.stack(core_terms), 'wide', scatter_dimension=1, tile...  58.4 us
    reduce_scatter x1, waiting for transfers between devices, body(): lax.psum_scatter(tail_acc[None], 'wide', scatter_dimension=1, tiled=True)  19.9 us
    reduce_scatter x1, waiting for transfers between devices, body(): lax.psum_scatter(head_acc, ('tail', 'sub'), scatter_dimension=0, tiled=True)  19.8 us
    psum x1, waiting for transfers between devices, body(): score_tile = lax.psum(partial_score, 'sub')  17.4 us
    reduce_scatter x1, waiting for transfers between devices, body(): lax.psum_scatter(combined, 'tail', scatter_dimension=0, tiled=True)  13.6 us
    dot_general x8, matrix products, body(): lax.dot_general(head_embed, weighted, (((0,), (0,)), ((), ())), precision...  11.5 us
    dot_general x8, matrix products, body(): lax.dot_general(residual, projected, (((0,), (0,)), ((), ())), precision=...  10.6 us
  transfers between devices with their start and end apart: 6, of which 6 were waited for; matrix products, arithmetic and copies ran while one was open for 7% of the time, Pallas kernels for 0%

commit v1 on v0

--- a/solution.py
+++ b/solution.py
@@ -1,9 +1,279 @@
+import functools
 import math
 
 import jax
 import jax.numpy as jnp
 from jax import lax
+from jax.experimental import pallas as pl
+from jax.experimental.pallas import tpu as pltpu
 from jax.sharding import PartitionSpec as P
+
+MESH = pl.DeviceIdType.MESH
+F32 = jnp.float32
+BF16 = jnp.bfloat16
+NN = (((1,), (0,)), ((), ()))
+NT = (((1,), (1,)), ((), ()))
+
+
+def split(value):
+    high = value.astype(BF16)
+    return high, (value - high.astype(F32)).astype(BF16)
+
+
+def dot3(a, b, dims):
+    one = lambda x, y: lax.dot_general(x, y, dims, preferred_element_type=F32)
+    return one(a[0], b[0]) + (one(a[0], b[1]) + one(a[1], b[0]))
+
+
+def kernel(
+    wides, tails, per_tail, scales,
+    lists, head, tail, core, labels,
+    head_out, tail_out, core_out,
+    heads, count_out, count_in, core_far, tail_far, tail_x, rho_z, rho_x,
+    tp_out, tp_in, tp_sum, tp_z, hg, hg_x, hg_sum, hg_z, g_out, g_in,
+    sib_send, sib_recv, z_send, z_recv, x_send, x_recv,
+):
+    w, t, s = lax.axis_index("wide"), lax.axis_index("tail"), lax.axis_index("sub")
+    sibling = {"sub": 1 - s}
+    z_peers = [lax.rem(w + k, wides) for k in range(1, wides)]
+    x_peers = [lax.rem(t + k, tails) for k in range(1, tails)]
+    part = heads.shape[2]
+    width = heads.shape[3]
+    tail_rows, half = tail.shape
+    slots = labels.shape[1]
+    row_count = tails * wides * part
+
+    def copy(src, dst, send, recv, device):
+        return pltpu.make_async_remote_copy(
+            src_ref=src, dst_ref=dst, send_sem=send, recv_sem=recv,
+            device_id=device, device_id_type=MESH,
+        )
+
+    sent = []
+
+    def put(src, dst, send, recv, device):
+        job = copy(src, dst, send, recv, device)
+        job.start()
+        sent.append(job)
+
+    def arrived(dst, send, recv, device):
+        copy(dst, dst, send, recv, device).wait_recv()
+
+    def put_sub(kind, src, dst):
+        put(src, dst, sib_send.at[kind], sib_recv.at[kind], sibling)
+
+    def take_sub(kind, dst):
+        arrived(dst, sib_send.at[kind], sib_recv.at[kind], sibling)
+
+    def put_z(kind, k, src, dst):
+        put(src, dst, z_send.at[kind, k], z_recv.at[kind, w], {"wide": z_peers[k]})
+
+    def take_z(kind, p, dst):
+        arrived(dst, z_send.at[kind, 0], z_recv.at[kind, p], {"wide": z_peers[0]})
+
+    def put_x(kind, k, src, dst):
+        put(src, dst, x_send.at[kind, k], x_recv.at[kind, t], {"tail": x_peers[k]})
+
+    def take_x(kind, p, dst):
+        arrived(dst, x_send.at[kind, 0], x_recv.at[kind, p], {"tail": x_peers[0]})
+
+    barrier = pltpu.get_barrier_semaphore()
+    partners = [sibling] + [{"wide": p} for p in z_peers] + [{"tail": p} for p in x_peers]
+    for device in partners:
+        pl.semaphore_signal(barrier, inc=1, device_id=device, device_id_type=MESH)
+    for tau in range(tails):
+        start = pl.multiple_of((tau * 2 + s) * part, part)
+        heads[tau, w] = head[pl.ds(start, part), :]
+    pl.semaphore_wait(barrier, len(partners))
+
+    for k in reversed(range(len(z_peers))):
+        put_z(0, k, heads.at[:, w], heads.at[:, w])
+    put_sub(0, core.at[0], core_far)
+    put_sub(1, tail, tail_far)
+    for k in range(len(x_peers)):
+        put_x(0, k, tail, tail_x.at[t, 0])
+
+    shape = (wides, part, part * slots)
+    lane = lax.broadcasted_iota(jnp.int32, shape, 2)
+    offset = lane - slots * lax.broadcasted_iota(jnp.int32, shape, 1)
+    listed = jnp.full(shape, -1, jnp.int32)
+    for j in range(slots):
+        listed = jnp.where(offset == j, lists[0, j], listed)
+    picks = jnp.where(listed == lax.broadcasted_iota(jnp.int32, shape, 0), 1.0, 0.0)
+    picks = picks.reshape(wides * part, part * slots).astype(BF16)
+    for tau in range(tails):
+        start = (tau * 2 + s) * part
+        block = labels[pl.ds(start, part)].reshape(part * slots, tail_rows)
+        counts = lax.dot_general(
+            picks, block.astype(F32).astype(BF16), NN, preferred_element_type=F32
+        )
+        count_out[:, tau] = counts.reshape(wides, part, tail_rows)
+    for k, p in enumerate(z_peers):
+        put_z(1, k, count_out.at[p], count_in.at[:, w])
+    count_in[:, w] = count_out[w]
+    uses = jnp.float32(0.0)
+    for j in range(slots):
+        uses = uses + (lists[0, j] == w).astype(F32)
+
+    core_near = split(core[0])
+    tail_near = split(tail[...])
+    take_sub(0, core_far)
+    core_away = split(core_far[...])
+    take_sub(1, tail_far)
+    tail_away = split(tail_far[...])
+    for p in z_peers:
+        take_z(0, p, heads.at[:, p])
+    all_heads = split(heads[...].reshape(row_count, width))
+    near = dot3(all_heads, core_near, NN)
+    away = dot3(all_heads, core_away, NN)
+    near_pair, away_pair = split(near), split(away)
+    score = dot3(near_pair, tail_near, NT) + dot3(away_pair, tail_away, NT)
+    chance = 1.0 / (1.0 + jnp.exp(-score))
+    for p in z_peers:
+        take_z(1, p, count_in.at[:, p])
+    rho = uses * chance - count_in[...].reshape(row_count, tail_rows)
+    rho_z[w] = rho
+    for k in reversed(range(len(z_peers))):
+        put_z(2, k, rho_z.at[w], rho_z.at[w])
+
+    for k, p in enumerate(x_peers):
+        take_x(0, p, tail_x.at[p, 0])
+        put_sub(2 + k, tail_x.at[p, 0], tail_x.at[p, 1])
+    kind = 1 + tails
+
+    rho_pair = split(rho)
+    weighted = (
+        split(dot3(rho_pair, tail_near, NN)),
+        split(dot3(rho_pair, tail_away, NN)),
+    )
+    head_term = dot3(weighted[0], core_near, NT) + dot3(weighted[1], core_away, NT)
+    hg[...] = head_term.reshape(tails, wides, part, width)
+    for k, p in enumerate(x_peers):
+        put_x(1, k, hg.at[p], hg_x.at[t])
+
+    turned = split(rho.T)
+    tp_out[...] = dot3(turned, away_pair, NN)
+    put_sub(kind, tp_out, tp_in)
+    tail_term = dot3(turned, near_pair, NN)
+
+    total = hg[t]
+    for p in x_peers:
+        take_x(1, p, hg_x.at[p])
+        total = total + hg_x[p]
+    hg_sum[...] = total
+    for k, p in enumerate(z_peers):
+        put_z(4, k, hg_sum.at[p], hg_z.at[w])
+    take_sub(kind, tp_in)
+    tp_sum[...] = (tail_term + tp_in[...]).reshape(wides, tail_rows // wides, half)
+    for k, p in enumerate(z_peers):
+        put_z(3, k, tp_sum.at[p], tp_z.at[w])
+
+    def take_rho(r):
+        @pl.when(r != w)
+        def _():
+            take_z(2, r, rho_z.at[r])
+
+    for k, p in enumerate(x_peers):
+        for i in range(per_tail):
+            r = p * per_tail + i
+            take_rho(r)
+            put_x(2 + i, k, rho_z.at[r], rho_x.at[t, i])
+    for i in range(per_tail):
+        take_rho(t * per_tail + i)
+    for k, p in enumerate(x_peers):
+        take_sub(2 + k, tail_x.at[p, 1])
+    tail_all = [
+        split(jnp.concatenate([own[...]] + [tail_x[p, side] for p in x_peers], axis=0))
+        for side, own in enumerate((tail, tail_far))
+    ]
+    columns = width // wides
+    at = pl.multiple_of(w * columns, columns)
+    turned_heads = split(heads[:, :, :, pl.ds(at, columns)].reshape(row_count, columns).T)
+    kept = []
+    for i in range(per_tail):
+        for p in x_peers:
+            take_x(2 + i, p, rho_x.at[p, i])
+        rhos = [rho_z[t * per_tail + i]] + [rho_x[p, i] for p in x_peers]
+        rhos = split(jnp.concatenate(rhos, axis=1))
+        g_out[i] = dot3(turned_heads, split(dot3(rhos, tail_all[1], NN)), NN)
+        put_sub(kind + 1 + i, g_out.at[i], g_in.at[i])
+        core_out[i] = dot3(turned_heads, split(dot3(rhos, tail_all[0], NN)), NN)
+
+    total = hg_sum[w]
+    for p in z_peers:
+        take_z(4, p, hg_z.at[p])
+        total = total + hg_z[p]
+    head_out[...] = total * scales[0]
+    total = tp_sum[w]
+    for p in z_peers:
+        take_z(3, p, tp_z.at[p])
+        total = total + tp_z[p]
+    tail_out[0] = total * scales[1]
+    for i in range(per_tail):
+        take_sub(kind + 1 + i, g_in.at[i])
+        core_out[i] = (core_out[i] + g_in[i]) * scales[2]
+    for job in sent:
+        job.wait_send()
+
+
+def fused(wides, tails, head_embed, tail_embed, core_mats, labels, core_lists):
+    rows, width = head_embed.shape
+    tail_rows, half = tail_embed.shape
+    slots = core_lists.shape[1]
+    part = rows // (2 * tails)
+    per_tail = wides // tails
+    count = tails * wides * part
+    columns = width // wides
+    block = tail_rows // wides
+    scales = (
+        1.0 / math.sqrt(slots * tail_rows * tails),
+        1.0 / math.sqrt(slots * rows * wides),
+        1.0 / math.sqrt(rows * wides * tail_rows),
+    )
+    vmem = pl.BlockSpec(memory_space=pltpu.VMEM)
+    buffer = lambda *shape: pltpu.VMEM(shape, F32)
+    sub_kinds = 1 + tails + 1 + per_tail
+    x_kinds = 2 + per_tail
+    sems = pltpu.SemaphoreType.DMA
+    return pl.pallas_call(
+        functools.partial(kernel, wides, tails, per_tail, scales),
+        out_shape=(
+            jax.ShapeDtypeStruct((part, width), F32),
+            jax.ShapeDtypeStruct((1, block, half), F32),
+            jax.ShapeDtypeStruct((per_tail, columns, half), F32),
+        ),
+        in_specs=[pl.BlockSpec(memory_space=pltpu.SMEM)] + [vmem] * 4,
+        out_specs=(vmem, vmem, vmem),
+        scratch_shapes=[
+            buffer(tails, wides, part, width),
+            buffer(wides, tails, part, tail_rows),
+            buffer(tails, wides, part, tail_rows),
+            buffer(width, half),
+            buffer(tail_rows, half),
+            buffer(tails, 2, tail_rows, half),
+            buffer(wides, count, tail_rows),
+            buffer(tails, per_tail, count, tail_rows),
+            buffer(tail_rows, half),
+            buffer(tail_rows, half),
+            buffer(wides, block, half),
+            buffer(wides, block, half),
+            buffer(tails, wides, part, width),
+            buffer(tails, wides, part, width),
+            buffer(wides, part, width),
+            buffer(wides, part, width),
+            buffer(per_tail, columns, half),
+            buffer(per_tail, columns, half),
+            sems((sub_kinds,)),
+            sems((sub_kinds,)),
+            sems((5, wides)),
+            sems((5, wides)),
+            sems((x_kinds, tails)),
+            sems((x_kinds, tails)),
+        ],
+        compiler_params=pltpu.CompilerParams(
+            collective_id=0, has_side_effects=True, vmem_limit_bytes=40 * 2**20
+        ),
+    )(core_lists, head_embed, tail_embed, core_mats, labels)
 
 
 def broadcast(value, axis, source):
@@ -11,7 +281,7 @@
     return lax.psum(kept, axis)
 
 
-def body(head_embed, tail_embed, core_mats, labels, core_lists):
+def collective(head_embed, tail_embed, core_mats, labels, core_lists):
     highest = lax.Precision.HIGHEST
     slot_count = core_lists.shape[1]
     half_width = tail_embed.shape[1]
@@ -69,6 +339,22 @@
 
 
 def solution(mesh):
+    wides, tails, subs = (mesh.shape[name] for name in ("wide", "tail", "sub"))
+
+    def body(head_embed, tail_embed, core_mats, labels, core_lists):
+        rows, width = head_embed.shape
+        fits = (
+            subs == 2
+            and core_mats.shape[0] == 1
+            and wides % tails == 0
+            and rows % (16 * tails) == 0
+            and tail_embed.shape[0] % (8 * wides) == 0
+            and width % (128 * wides) == 0
+        )
+        if fits:
+            return fused(wides, tails, head_embed, tail_embed, core_mats, labels, core_lists)
+        return collective(head_embed, tail_embed, core_mats, labels, core_lists)
+
     in_specs = (
         P(("groups", "wide"), None),
         P(("groups", "tail"), "sub"),

time: 379 us -> 36.5 us (0.10)
  the two profiles are of different devices: /device:TPU:0 before, /device:TPU:3 now
where the time goes in v1:
time: 36.5 us; the launch traced here: 36.2 us
  Pallas kernels  29.2 us (80%)
  local copies, waits for them, and re-layouts  6.38 us (17%)
  between operations  0.65 us (2%)
    pallas_call x1, Pallas kernels, fused(): pl.pallas_call(functools.partial(kernel, wides, tails, per_tail, scales),...  29.2 us
    unnamed x13, local copies, waits for them, and re-layouts  6.38 us

profile of v1, /device:TPU:3, one launch (start us, length us, event | category | flops | bytes accessed | tf_op | source)
XLA Modules:
  0.0 36.2 jit_solution(16473959300590640032)
XLA Ops:
  0.6 0.0 copy-start
  0.6 1.0 %copy-done = f32[1,512,256]{2,1,0:T(8,128)S(1)} copy-done((f32[1,512,256]{2,1,0:T(8,128)S(1)}, f32[1,512,256]{2,1,0:T(8,128)}, u32[]{:S(2)}) %copy-start) | copy-done | bytes 524312
  1.7 0.0 copy-start.1
  1.7 0.9 %copy-done.1 = s32[64,8,128]{2,1,0:T(8,128)S(1)} copy-done((s32[64,8,128]{2,1,0:T(8,128)S(1)}, s32[64,8,128]{2,1,0:T(8,128)}, u32[]{:S(2)}) %copy-start.1) | copy-done | bytes 262168
  2.6 0.0 copy-start.2
  2.6 0.9 %copy-done.2 = f32[64,512]{1,0:T(8,128)S(1)} copy-done((f32[64,512]{1,0:T(8,128)S(1)}, f32[64,512]{1,0:T(8,128)}, u32[]{:S(2)}) %copy-start.2) | copy-done | bytes 131096
  3.5 0.0 copy-start.3
  3.5 0.9 %copy-done.3 = f32[128,256]{1,0:T(8,128)S(1)} copy-done((f32[128,256]{1,0:T(8,128)S(1)}, f32[128,256]{1,0:T(8,128)}, u32[]{:S(2)}) %copy-start.3) | copy-done | bytes 131096
  4.4 0.0 copy-start.4
  4.4 0.7 %copy-done.4 = s32[1,8]{1,0:T(1,128)S(1)} copy-done((s32[1,8]{1,0:T(1,128)S(1)}, s32[1,8]{1,0:T(1,128)}, u32[]{:S(2)}) %copy-start.4) | copy-done | bytes 56
  5.1 29.2 %shard_map.76 = (f32[16,512]{1,0:T(8,128)S(1)}, f32[1,32,256]{2,1,0:T(8,128)S(1)}, f32[2,128,256]{2,1,0:T(8,128)S(1)}) custom-call(s32[1,8]{1,0:T(1,128)S(1)} %copy-done.4, f32[64,512]{1,0:T(8,128)S(1)} %copy-done.2, f32[128,256]{1,0:T(8,128)S(1)} %copy-done.3, f32[1,512,256]{2,1,0:T(8,128)S(1)} %copy-done, s32[64,8,128]{2,1,0:T(8,128)S(1)} %copy-done.1), custom_call_target="tpu_custom_call" | custom-call | tf_op jit(solution)/shard_map/pallas_call | solution.py:238
  34.3 0.6 %copy.11 = f32[16,512]{1,0:T(8,128)} copy(f32[16,512]{1,0:T(8,128)S(1)} %get-tuple-element.6) | data formatting | bytes 65536
  34.9 0.6 %copy.12 = f32[1,32,256]{2,1,0:T(8,128)} copy(f32[1,32,256]{2,1,0:T(8,128)S(1)} %get-tuple-element.7) | data formatting | bytes 65536
  35.5 0.7 %copy.13 = f32[2,128,256]{2,1,0:T(8,128)} copy(f32[2,128,256]{2,1,0:T(8,128)S(1)} %get-tuple-element.8) | data formatting | bytes 524288
Async XLA Ops:
  0.6 1.0 %copy-start = (f32[1,512,256]{2,1,0:T(8,128)S(1)}, f32[1,512,256]{2,1,0:T(8,128)}, u32[]{:S(2)}) copy-start(f32[1,512,256]{2,1,0:T(8,128)} %core.1) | copy-start | bytes 1572868
  1.7 0.9 %copy-start.1 = (s32[64,8,128]{2,1,0:T(8,128)S(1)}, s32[64,8,128]{2,1,0:T(8,128)}, u32[]{:S(2)}) copy-start(s32[64,8,128]{2,1,0:T(8,128)} %labels.1) | copy-start | bytes 786436
  2.6 0.9 %copy-start.2 = (f32[64,512]{1,0:T(8,128)S(1)}, f32[64,512]{1,0:T(8,128)}, u32[]{:S(2)}) copy-start(f32[64,512]{1,0:T(8,128)} %head.1) | copy-start | bytes 393220
  3.5 0.9 %copy-start.3 = (f32[128,256]{1,0:T(8,128)S(1)}, f32[128,256]{1,0:T(8,128)}, u32[]{:S(2)}) copy-start(f32[128,256]{1,0:T(8,128)} %tail.1) | copy-start | bytes 393220
  4.4 0.7 %copy-start.4 = (s32[1,8]{1,0:T(1,128)S(1)}, s32[1,8]{1,0:T(1,128)}, u32[]{:S(2)}) copy-start(s32[1,8]{1,0:T(1,128)} %lists.1) | copy-start | bytes 100

commit v2 on v1

--- a/solution.py
+++ b/solution.py
@@ -27,11 +27,13 @@
 
 def kernel(
     wides, tails, per_tail, scales,
-    lists, head, tail, core, labels,
+    lists_hbm, head_hbm, tail_hbm, core_hbm, labels_hbm,
     head_out, tail_out, core_out,
-    heads, count_out, count_in, core_far, tail_far, tail_x, rho_z, rho_x,
-    tp_out, tp_in, tp_sum, tp_z, hg, hg_x, hg_sum, hg_z, g_out, g_in,
-    sib_send, sib_recv, z_send, z_recv, x_send, x_recv,
+    lists, labels, tail, core,
+    heads, count_out, count_in, core_far, tail_far, tail_x,
+    q_all, q_in, q_sum, q_z, q_x,
+    tp_out, tp_in, tp_sum, tp_z, hg, hg_x, hg_sum, hg_z,
+    own_sem, sib_send, sib_recv, z_send, z_recv, x_send, x_recv,
 ):
     w, t, s = lax.axis_index("wide"), lax.axis_index("tail"), lax.axis_index("sub")
     sibling = {"sub": 1 - s}
@@ -40,8 +42,9 @@
     part = heads.shape[2]
     width = heads.shape[3]
     tail_rows, half = tail.shape
-    slots = labels.shape[1]
+    slots = labels.shape[2]
     row_count = tails * wides * part
+    columns = width // wides
 
     def copy(src, dst, send, recv, device):
         return pltpu.make_async_remote_copy(
@@ -81,18 +84,29 @@
     partners = [sibling] + [{"wide": p} for p in z_peers] + [{"tail": p} for p in x_peers]
     for device in partners:
         pl.semaphore_signal(barrier, inc=1, device_id=device, device_id_type=MESH)
-    for tau in range(tails):
-        start = pl.multiple_of((tau * 2 + s) * part, part)
-        heads[tau, w] = head[pl.ds(start, part), :]
+    own = [
+        pltpu.make_async_copy(src, dst, own_sem.at[i])
+        for i, (src, dst) in enumerate((
+            (lists_hbm, lists),
+            (labels_hbm.at[:, s], labels),
+            (head_hbm.at[:, s], heads.at[:, w]),
+            (core_hbm.at[0], core),
+            (tail_hbm, tail),
+        ))
+    ]
+    for job in own:
+        job.start()
     pl.semaphore_wait(barrier, len(partners))
 
     for k in reversed(range(len(z_peers))):
-        put_z(0, k, heads.at[:, w], heads.at[:, w])
-    put_sub(0, core.at[0], core_far)
-    put_sub(1, tail, tail_far)
+        put_z(0, k, head_hbm.at[:, s], heads.at[:, w])
+    put_sub(0, core_hbm.at[0], core_far)
+    put_sub(1, tail_hbm, tail_far)
     for k in range(len(x_peers)):
-        put_x(0, k, tail, tail_x.at[t, 0])
-
+        put_x(0, k, tail_hbm, tail_x.at[t])
+
+    own[0].wait()
+    own[1].wait()
     shape = (wides, part, part * slots)
     lane = lax.broadcasted_iota(jnp.int32, shape, 2)
     offset = lane - slots * lax.broadcasted_iota(jnp.int32, shape, 1)
@@ -102,8 +116,7 @@
     picks = jnp.where(listed == lax.broadcasted_iota(jnp.int32, shape, 0), 1.0, 0.0)
     picks = picks.reshape(wides * part, part * slots).astype(BF16)
     for tau in range(tails):
-        start = (tau * 2 + s) * part
-        block = labels[pl.ds(start, part)].reshape(part * slots, tail_rows)
+        block = labels[tau].reshape(part * slots, tail_rows)
         counts = lax.dot_general(
             picks, block.astype(F32).astype(BF16), NN, preferred_element_type=F32
         )
@@ -115,37 +128,41 @@
     for j in range(slots):
         uses = uses + (lists[0, j] == w).astype(F32)
 
-    core_near = split(core[0])
+    own[3].wait()
+    own[4].wait()
+    core_near = split(core[...])
     tail_near = split(tail[...])
     take_sub(0, core_far)
     core_away = split(core_far[...])
     take_sub(1, tail_far)
     tail_away = split(tail_far[...])
+    own[2].wait()
     for p in z_peers:
         take_z(0, p, heads.at[:, p])
-    all_heads = split(heads[...].reshape(row_count, width))
-    near = dot3(all_heads, core_near, NN)
-    away = dot3(all_heads, core_away, NN)
-    near_pair, away_pair = split(near), split(away)
+    head_rows = heads[...].reshape(row_count, width)
+    all_heads = split(head_rows)
+    near_pair = split(dot3(all_heads, core_near, NN))
+    away_pair = split(dot3(all_heads, core_away, NN))
     score = dot3(near_pair, tail_near, NT) + dot3(away_pair, tail_away, NT)
+    turned_heads = split(head_rows.T)
     chance = 1.0 / (1.0 + jnp.exp(-score))
     for p in z_peers:
         take_z(1, p, count_in.at[:, p])
     rho = uses * chance - count_in[...].reshape(row_count, tail_rows)
-    rho_z[w] = rho
-    for k in reversed(range(len(z_peers))):
-        put_z(2, k, rho_z.at[w], rho_z.at[w])
-
-    for k, p in enumerate(x_peers):
-        take_x(0, p, tail_x.at[p, 0])
-        put_sub(2 + k, tail_x.at[p, 0], tail_x.at[p, 1])
-    kind = 1 + tails
-
     rho_pair = split(rho)
+
+    q_all[...] = dot3(turned_heads, rho_pair, NN).reshape(wides, 2, columns // 2, tail_rows)
+    put_sub(3, q_all.at[:, 1 - s], q_in)
+
     weighted = (
         split(dot3(rho_pair, tail_near, NN)),
         split(dot3(rho_pair, tail_away, NN)),
     )
+    take_sub(3, q_in)
+    q_sum[...] = q_all[:, s] + q_in[...]
+    for k in reversed(range(len(z_peers))):
+        put_z(2, k, q_sum.at[z_peers[k]], q_z.at[w, s])
+    q_z[w, s] = q_sum[w]
     head_term = dot3(weighted[0], core_near, NT) + dot3(weighted[1], core_away, NT)
     hg[...] = head_term.reshape(tails, wides, part, width)
     for k, p in enumerate(x_peers):
@@ -153,8 +170,23 @@
 
     turned = split(rho.T)
     tp_out[...] = dot3(turned, away_pair, NN)
-    put_sub(kind, tp_out, tp_in)
+    put_sub(2, tp_out, tp_in)
     tail_term = dot3(turned, near_pair, NN)
+
+    def take_q(r):
+        @pl.when(r != w)
+        def _():
+            take_z(2, r, q_z.at[r, s])
+
+    for k, p in enumerate(x_peers):
+        for i in range(per_tail):
+            r = p * per_tail + i
+            take_q(r)
+            put_x(2 + i, k, q_z.at[r, s], q_x.at[t, i, s])
+    for i in range(per_tail):
+        r = t * per_tail + i
+        take_q(r)
+        put_sub(4 + i, q_z.at[r, s], q_z.at[r, s])
 
     total = hg[t]
     for p in x_peers:
@@ -163,41 +195,34 @@
     hg_sum[...] = total
     for k, p in enumerate(z_peers):
         put_z(4, k, hg_sum.at[p], hg_z.at[w])
-    take_sub(kind, tp_in)
+    take_sub(2, tp_in)
     tp_sum[...] = (tail_term + tp_in[...]).reshape(wides, tail_rows // wides, half)
     for k, p in enumerate(z_peers):
         put_z(3, k, tp_sum.at[p], tp_z.at[w])
 
-    def take_rho(r):
-        @pl.when(r != w)
-        def _():
-            take_z(2, r, rho_z.at[r])
-
+    for k, p in enumerate(x_peers):
+        take_x(0, p, tail_x.at[p])
+    tail_all = split(jnp.concatenate([tail[...]] + [tail_x[p] for p in x_peers], axis=0))
+    base = 4 + per_tail
     for k, p in enumerate(x_peers):
         for i in range(per_tail):
-            r = p * per_tail + i
-            take_rho(r)
-            put_x(2 + i, k, rho_z.at[r], rho_x.at[t, i])
+            take_x(2 + i, p, q_x.at[p, i, s])
+            put_sub(base + k * per_tail + i, q_x.at[p, i, s], q_x.at[p, i, s])
     for i in range(per_tail):
-        take_rho(t * per_tail + i)
+        take_sub(4 + i, q_z.at[t * per_tail + i, 1 - s])
     for k, p in enumerate(x_peers):
-        take_sub(2 + k, tail_x.at[p, 1])
-    tail_all = [
-        split(jnp.concatenate([own[...]] + [tail_x[p, side] for p in x_peers], axis=0))
-        for side, own in enumerate((tail, tail_far))
+        for i in range(per_tail):
+            take_sub(base + k * per_tail + i, q_x.at[p, i, 1 - s])
+    rows = [
+        jnp.concatenate(
+            [block.reshape(columns, tail_rows) for block in
+             [q_z[t * per_tail + i]] + [q_x[p, i] for p in x_peers]],
+            axis=1,
+        )
+        for i in range(per_tail)
     ]
-    columns = width // wides
-    at = pl.multiple_of(w * columns, columns)
-    turned_heads = split(heads[:, :, :, pl.ds(at, columns)].reshape(row_count, columns).T)
-    kept = []
-    for i in range(per_tail):
-        for p in x_peers:
-            take_x(2 + i, p, rho_x.at[p, i])
-        rhos = [rho_z[t * per_tail + i]] + [rho_x[p, i] for p in x_peers]
-        rhos = split(jnp.concatenate(rhos, axis=1))
-        g_out[i] = dot3(turned_heads, split(dot3(rhos, tail_all[1], NN)), NN)
-        put_sub(kind + 1 + i, g_out.at[i], g_in.at[i])
-        core_out[i] = dot3(turned_heads, split(dot3(rhos, tail_all[0], NN)), NN)
+    grads = dot3(split(jnp.concatenate(rows, axis=0)), tail_all, NN)
+    core_out[...] = grads.reshape(per_tail, columns, half) * scales[2]
 
     total = hg_sum[w]
     for p in z_peers:
@@ -209,11 +234,20 @@
         take_z(3, p, tp_z.at[p])
         total = total + tp_z[p]
     tail_out[0] = total * scales[1]
-    for i in range(per_tail):
-        take_sub(kind + 1 + i, g_in.at[i])
-        core_out[i] = (core_out[i] + g_in[i]) * scales[2]
     for job in sent:
         job.wait_send()
+
+
+def store(count, *refs):
+    sources, targets, sems = refs[:count], refs[count:2 * count], refs[2 * count]
+    jobs = [
+        pltpu.make_async_copy(source, target, sems.at[i])
+        for i, (source, target) in enumerate(zip(sources, targets))
+    ]
+    for job in jobs:
+        job.start()
+    for job in jobs:
+        job.wait()
 
 
 def fused(wides, tails, head_embed, tail_embed, core_mats, labels, core_lists):
@@ -222,7 +256,6 @@
     slots = core_lists.shape[1]
     part = rows // (2 * tails)
     per_tail = wides // tails
-    count = tails * wides * part
     columns = width // wides
     block = tail_rows // wides
     scales = (
@@ -230,29 +263,38 @@
         1.0 / math.sqrt(slots * rows * wides),
         1.0 / math.sqrt(rows * wides * tail_rows),
     )
+    hbm = pl.BlockSpec(memory_space=pltpu.HBM)
     vmem = pl.BlockSpec(memory_space=pltpu.VMEM)
     buffer = lambda *shape: pltpu.VMEM(shape, F32)
-    sub_kinds = 1 + tails + 1 + per_tail
+    sub_kinds = 4 + per_tail * tails
     x_kinds = 2 + per_tail
     sems = pltpu.SemaphoreType.DMA
-    return pl.pallas_call(
+    shapes = (
+        jax.ShapeDtypeStruct((part, width), F32),
+        jax.ShapeDtypeStruct((1, block, half), F32),
+        jax.ShapeDtypeStruct((per_tail, columns, half), F32),
+    )
+    results = pl.pallas_call(
         functools.partial(kernel, wides, tails, per_tail, scales),
-        out_shape=(
-            jax.ShapeDtypeStruct((part, width), F32),
-            jax.ShapeDtypeStruct((1, block, half), F32),
-            jax.ShapeDtypeStruct((per_tail, columns, half), F32),
-        ),
-        in_specs=[pl.BlockSpec(memory_space=pltpu.SMEM)] + [vmem] * 4,
-        out_specs=(vmem, vmem, vmem),
+        out_shape=shapes,
+        in_specs=[hbm] * 5,
+        out_specs=(vmem,) * 3,
         scratch_shapes=[
+            pltpu.SMEM((1, slots), jnp.int32),
+            pltpu.VMEM((tails, part, slots, tail_rows), jnp.int32),
+            buffer(tail_rows, half),
+            buffer(width, half),
             buffer(tails, wides, part, width),
             buffer(wides, tails, part, tail_rows),
             buffer(tails, wides, part, tail_rows),
             buffer(width, half),
             buffer(tail_rows, half),
-            buffer(tails, 2, tail_rows, half),
-            buffer(wides, count, tail_rows),
-            buffer(tails, per_tail, count, tail_rows),
+            buffer(tails, tail_rows, half),
+            buffer(wides, 2, columns // 2, tail_rows),
+            buffer(wides, columns // 2, tail_rows),
+            buffer(wides, columns // 2, tail_rows),
+            buffer(wides, 2, columns // 2, tail_rows),
+            buffer(tails, per_tail, 2, columns // 2, tail_rows),
             buffer(tail_rows, half),
             buffer(tail_rows, half),
             buffer(wides, block, half),
@@ -261,8 +303,7 @@
             buffer(tails, wides, part, width),
             buffer(wides, part, width),
             buffer(wides, part, width),
-            buffer(per_tail, columns, half),
-            buffer(per_tail, columns, half),
+            sems((5,)),
             sems((sub_kinds,)),
             sems((sub_kinds,)),
             sems((5, wides)),
@@ -273,7 +314,23 @@
         compiler_params=pltpu.CompilerParams(
             collective_id=0, has_side_effects=True, vmem_limit_bytes=40 * 2**20
         ),
-    )(core_lists, head_embed, tail_embed, core_mats, labels)
+    )(*[
+        pltpu.with_memory_space_constraint(value, pltpu.HBM)
+        for value in (
+            core_lists,
+            head_embed.reshape(tails, 2, part, width),
+            tail_embed,
+            core_mats,
+            labels.reshape(tails, 2, part, slots, tail_rows),
+        )
+    ])
+    return pl.pallas_call(
+        functools.partial(store, len(shapes)),
+        out_shape=shapes,
+        in_specs=[vmem] * 3,
+        out_specs=(hbm,) * 3,
+        scratch_shapes=[sems((3,))],
+    )(*[pltpu.with_memory_space_constraint(value, pltpu.VMEM) for value in results])
 
 
 def broadcast(value, axis, source):

time: 36.5 us -> 30.3 us (0.83)
  the two profiles are of different devices: /device:TPU:3 before, /device:TPU:0 now
where the time goes in v2:
time: 30.3 us; the launch traced here: 30.1 us
  Pallas kernels  29.5 us (97%)
  between operations  0.64 us (2%)
    pallas_call x1, Pallas kernels, fused(): pl.pallas_call(functools.partial(kernel, wides, tails, per_tail, scales),...  28.7 us
    pallas_call x1, Pallas kernels, fused(): pl.pallas_call(functools.partial(store, len(shapes)), out_shape=shapes, i...  0.75 us

profile of v2, /device:TPU:0, one launch (start us, length us, event | category | flops | bytes accessed | tf_op | source)
XLA Modules:
  0.0 30.1 jit_solution(8393474830457622433)
XLA Ops:
  0.6 28.7 %shard_map.76 = (f32[16,512]{1,0:T(8,128)S(1)}, f32[1,32,256]{2,1,0:T(8,128)S(1)}, f32[2,128,256]{2,1,0:T(8,128)S(1)}) custom-call(s32[1,8]{1,0:T(1,128)} %lists_hbm.1, f32[2,2,16,512]{3,2,1,0:T(8,128)} %bitcast.3, f32[128,256]{1,0:T(8,128)} %tail_hbm.1, f32[1,512,256]{2,1,0:T(8,128)} %core_hbm.1, s32[2,2,16,8,128]{4,3,2,1,0:T(8,128)} %bitcast.2), custom_call_target="tpu_custom_call" | custom-call | tf_op jit(solution)/shard_map/pallas_call | solution.py:277
  29.4 0.8 %shard_map.77 = (f32[16,512]{1,0:T(8,128)}, f32[1,32,256]{2,1,0:T(8,128)}, f32[2,128,256]{2,1,0:T(8,128)}) custom-call(f32[16,512]{1,0:T(8,128)S(1)} %get-tuple-element.6.refs_0_, f32[1,32,256]{2,1,0:T(8,128)S(1)} %get-tuple-element.7.refs_1_, f32[2,128,256]{2,1,0:T(8,128)S(1)} %get-tuple-element.8.refs_2_), custom_call_target="tpu_custom_call" | custom-call | tf_op jit(solution)/shard_map/pallas_call | solution.py:327

commit v3 on v2

--- a/solution.py
+++ b/solution.py
@@ -154,6 +154,10 @@
     q_all[...] = dot3(turned_heads, rho_pair, NN).reshape(wides, 2, columns // 2, tail_rows)
     put_sub(3, q_all.at[:, 1 - s], q_in)
 
+    turned = split(rho.T)
+    tp_out[...] = dot3(turned, away_pair, NN)
+    put_sub(2, tp_out, tp_in)
+
     weighted = (
         split(dot3(rho_pair, tail_near, NN)),
         split(dot3(rho_pair, tail_away, NN)),
@@ -168,11 +172,19 @@
     for k, p in enumerate(x_peers):
         put_x(1, k, hg.at[p], hg_x.at[t])
 
-    turned = split(rho.T)
-    tp_out[...] = dot3(turned, away_pair, NN)
-    put_sub(2, tp_out, tp_in)
     tail_term = dot3(turned, near_pair, NN)
-
+    take_sub(2, tp_in)
+    tp_sum[...] = (tail_term + tp_in[...]).reshape(wides, tail_rows // wides, half)
+    for k, p in enumerate(z_peers):
+        put_z(3, k, tp_sum.at[p], tp_z.at[w])
+
+    total = hg[t]
+    for p in x_peers:
+        take_x(1, p, hg_x.at[p])
+        total = total + hg_x[p]
+    hg_sum[...] = total
+    for k, p in enumerate(z_peers):
+        put_z(4, k, hg_sum.at[p], hg_z.at[w])
     def take_q(r):
         @pl.when(r != w)
         def _():
@@ -187,18 +199,6 @@
         r = t * per_tail + i
         take_q(r)
         put_sub(4 + i, q_z.at[r, s], q_z.at[r, s])
-
-    total = hg[t]
-    for p in x_peers:
-        take_x(1, p, hg_x.at[p])
-        total = total + hg_x[p]
-    hg_sum[...] = total
-    for k, p in enumerate(z_peers):
-        put_z(4, k, hg_sum.at[p], hg_z.at[w])
-    take_sub(2, tp_in)
-    tp_sum[...] = (tail_term + tp_in[...]).reshape(wides, tail_rows // wides, half)
-    for k, p in enumerate(z_peers):
-        put_z(3, k, tp_sum.at[p], tp_z.at[w])
 
     for k, p in enumerate(x_peers):
         take_x(0, p, tail_x.at[p])

time: 30.3 us -> 28.2 us (0.931)
  Pallas kernels: 29.5 us -> 27.4 us
    pallas_call x1, Pallas kernels: 28.7 us -> 26.6 us  [fused(): pl.pallas_call(functools.partial(kernel, wides, tails, per_tail, scales),...]
where the time goes in v3:
time: 28.2 us; the launch traced here: 28 us
  Pallas kernels  27.4 us (97%)
  between operations  0.64 us (2%)
    pallas_call x1, Pallas kernels, fused(): pl.pallas_call(functools.partial(kernel, wides, tails, per_tail, scales),...  26.6 us
    pallas_call x1, Pallas kernels, fused(): pl.pallas_call(functools.partial(store, len(shapes)), out_shape=shapes, i...  0.75 us

profile of v3, /device:TPU:0, one launch (start us, length us, event | category | flops | bytes accessed | tf_op | source)
XLA Modules:
  0.0 28.0 jit_solution(4376735710195719123)
XLA Ops:
  0.6 26.6 %shard_map.76 = (f32[16,512]{1,0:T(8,128)S(1)}, f32[1,32,256]{2,1,0:T(8,128)S(1)}, f32[2,128,256]{2,1,0:T(8,128)S(1)}) custom-call(s32[1,8]{1,0:T(1,128)} %lists_hbm.1, f32[2,2,16,512]{3,2,1,0:T(8,128)} %bitcast.3, f32[128,256]{1,0:T(8,128)} %tail_hbm.1, f32[1,512,256]{2,1,0:T(8,128)} %core_hbm.1, s32[2,2,16,8,128]{4,3,2,1,0:T(8,128)} %bitcast.2), custom_call_target="tpu_custom_call" | custom-call | tf_op jit(solution)/shard_map/pallas_call | solution.py:277
  27.3 0.8 %shard_map.77 = (f32[16,512]{1,0:T(8,128)}, f32[1,32,256]{2,1,0:T(8,128)}, f32[2,128,256]{2,1,0:T(8,128)}) custom-call(f32[16,512]{1,0:T(8,128)S(1)} %get-tuple-element.6.refs_0_, f32[1,32,256]{2,1,0:T(8,128)S(1)} %get-tuple-element.7.refs_1_, f32[2,128,256]{2,1,0:T(8,128)S(1)} %get-tuple-element.8.refs_2_), custom_call_target="tpu_custom_call" | custom-call | tf_op jit(solution)/shard_map/pallas_call | solution.py:327
